TPU v7x, 32 devices: a whole 2x2x4 slice. The times are simulated.
32 devices in a mesh: loop: 8 (over y, x, core), tp: 4 (over z).
Axes of the slice: x: 2, y: 2, z: 4, core: 2. Of those that a mesh axis runs over, the one named last changes fastest.
Arguments:
- tokens: bfloat16 [2048, 4096], P('loop', 'tp'), may hold values from -6 to 6
- out_grad: bfloat16 [2048, 6144], P('loop', 'tp'), may hold values from -6 to 6
- qkv_weight: bfloat16 [3, 4096, 6144], P(None, 'loop', 'tp'), may hold values from -0.09375 to 0.09375
- dest_row: int32 [2048], P('loop'), may hold values from 0 to 383, as said below
- loop_modality: int32 [8], replicated, may hold values from 0 to 2, as said below
Outputs:
- projected: bfloat16 [2048, 6144], P('loop', 'tp')
- input_grad: bfloat16 [2048, 4096], P('loop', 'tp')
- weight_grad: bfloat16 [3, 4096, 6144], P(None, 'loop', 'tp')
Inputs may be any that keep to these rules, and one draw needn't show every extreme that they name: `dest_row`: within each aligned block of 256 tokens the values are distinct, so at most 48 tokens of one block name one loop; in every draw some loop is named by exactly 48 tokens of every block. `loop_modality`: A quarter of the loops hold 0, half hold 1, a quarter hold 2.
All inputs are finite; a program needn't handle non-finite values.
Results may differ from a plain program's by a relative error of at most 0.014.
Values may be sent and summed in bfloat16 or wider, within the bound.
No kernel may reach another device: no remote copies, remote signals or barrier semaphores. Data moves between devices by JAX's collectives and lax.ppermute only.
A program may use at most 128 MiB of HBM per device.

v0:
```python
import math
import jax
import jax.numpy as jnp
from jax import lax
from jax.sharding import PartitionSpec as P


def per_device(tokens, out_grad, qkv_weight, dest_row, loop_modality):
    loop_count = lax.axis_size("loop")
    row_count, feature_part = tokens.shape
    kinds, block_rows, column_count = qkv_weight.shape
    capacity = 3 * row_count // (2 * loop_count)
    grad_scale = 1.0 / math.sqrt(row_count * loop_count)
    own_kind = loop_modality[dest_row // capacity]
    kind_of = lax.all_gather(own_kind, "loop", axis=0, tiled=True)
    grads = lax.all_gather(out_grad, "loop", axis=0, tiled=True)
    features = lax.all_gather(tokens, "tp", axis=1, tiled=True)
    rows = lax.all_to_all(features, "loop", split_axis=1, concat_axis=0, tiled=True)
    masks = [(kind_of == kind)[:, None] for kind in range(kinds)]
    term = sum(
        (
            lax.dot_general(
                jnp.where(masks[kind], grads, 0),
                qkv_weight[kind],
                (((1,), (1,)), ((), ())),
                preferred_element_type=jnp.float32,
            )
            for kind in range(kinds)
        )
    ).astype(jnp.bfloat16)
    term = lax.all_to_all(term, "loop", split_axis=0, concat_axis=1, tiled=True)
    input_grad = lax.psum_scatter(term, "tp", scatter_dimension=1, tiled=True)
    partial = sum(
        (
            jnp.dot(
                jnp.where(masks[kind], rows, 0),
                qkv_weight[kind],
                preferred_element_type=jnp.float32,
            )
            for kind in range(kinds)
        )
    ).astype(jnp.bfloat16)
    projected = lax.psum_scatter(partial, "loop", scatter_dimension=0, tiled=True)
    weight_grad = jnp.stack(
        [
            (
                lax.dot_general(
                    jnp.where(masks[kind], rows, 0),
                    grads,
                    (((0,), (0,)), ((), ())),
                    preferred_element_type=jnp.float32,
                )
                * grad_scale
            ).astype(jnp.bfloat16)
            for kind in range(kinds)
        ]
    )
    return (projected, input_grad, weight_grad)


def solution(mesh):
    placed = (P("loop", "tp"), P("loop", "tp"), P(None, "loop", "tp"), P("loop"), P())
    return jax.shard_map(
        per_device,
        mesh=mesh,
        in_specs=placed,
        out_specs=(P("loop", "tp"), P("loop", "tp"), P(None, "loop", "tp")),
        check_vma=False,
    )
```

profile of v0, /device:TPU:0, one launch (start us, length us, event | category | flops | bytes accessed | tf_op | source)
XLA Modules:
  0.0 278.5 jit_solution(15667492491029857206)
XLA Ops:
  7.2 0.0 all-gather.5.cloned.1.call-start
  7.2 2.0 copy.17
  9.3 0.0 all-gather.5.cloned.1.call-update
  9.3 0.0 all-gather.7.cloned.1.call-start
  9.3 0.7 all-gather.7.cloned.1.call-update
  10.0 48.5 %all-gather.5.cloned.1.call-done = bf16[256,4096]{0,1:T(8,128)(2,1)} async-done(((bf16[256,1024]{0,1:T(8,128)(2,1)}), bf16[256,4096]{0,1:T(8,128)(2,1)}) %all-gather.5.cloned.1.call-update) | async-done | bytes 2097168 | tf_op jit(solution)/shard_map/all_gather | solution.py:17
  58.5 3.7 %all-to-all-start = ((bf16[256,8,512]{0,2,1:T(8,128)(2,1)}), bf16[256,8,512]{0,2,1:T(8,128)(2,1)S(1)}, u32[]{:S(2)}, u32[]{:S(2)}) async-start(bf16[256,8,512]{0,2,1:T(8,128)(2,1)} %bitcast.68), calls=%async_computation | async-start | bytes 4194304 | tf_op jit(solution)/shard_map/all_to_all | solution.py:18
  62.2 0.0 reduce-scatter.3.cloned.1.call-start
  62.3 0.7 fusion.37
  63.0 5.2 %compare_select_fusion.1 = s32[256]{0:T(256)S(1)} fusion(s32[256]{0:T(256)S(1)} %copy-done.3, s32[]{:T(128)} %bitcast, s32[]{:T(128)} %bitcast.1, s32[]{:T(128)} %bitcast.2, s32[]{:T(128)} %bitcast.3, s32[]{:T(128)} %bitcast.4, s32[]{:T(128)} %bitcast.5, s32[]{:T(128)} %bitcast.6, s32[]{:T(128)} %bitcast.7), kind=kLoop, calls=%fused_computation.48 | loop fusion | flops 6400 | bytes 2080 | tf_op jit(solution)/shard_map/gather | solution.py:14
  68.1 32.2 %all-gather.1 = s32[8,1,256]{2,1,0:T(1,128)S(1)} all-gather(s32[1,1,256]{2,1,0:T(1,128)S(1)} %bitcast.75), channel_id=2, replica_groups=mesh['loop'=8,'tp'=4] {'loop'}, dimensions={0}, use_global_device_ids=true | all-gather | bytes 9216 | tf_op jit(solution)/shard_map/all_gather | solution.py:15
  100.3 2.8 %broadcast_select_fusion = (bf16[8,256,512]{1,2,0:T(8,128)(2,1)}, bf16[8,256,512]{1,2,0:T(8,128)(2,1)}, bf16[8,256,512]{1,2,0:T(8,128)(2,1)}) fusion(pred[8,256]{1,0:T(8,128)(4,1)S(1)} %bitcast.72, bf16[256,8,512]{0,2,1:T(8,128)(2,1)S(1)} %all-to-all-done, pred[8,256]{1,0:T(8,128)(4,1)S(1)} %bitcast.74, pred[8,256]{1,0:T(8,128)(4,1)S(1)} %bitcast.73), kind=kLoop, calls=%fused_computation.27 | loop fusion | flops 3145728 | bytes 8394752 | tf_op jit(solution)/shard_map/jit(_where)/select_n | solution.py:36
  103.2 3.9 %copy.20 = bf16[8,256,512]{2,1,0:T(8,128)(2,1)} copy(bf16[8,256,512]{1,2,0:T(8,128)(2,1)} %get-tuple-element.8) | data formatting | bytes 4194304 | tf_op jit(solution)/shard_map/jit(_where)/select_n | solution.py:36
  107.1 4.0 %copy.18 = bf16[8,256,512]{2,1,0:T(8,128)(2,1)} copy(bf16[8,256,512]{1,2,0:T(8,128)(2,1)} %get-tuple-element.7) | data formatting | bytes 4194304 | tf_op jit(solution)/shard_map/jit(_where)/select_n | solution.py:36
  111.1 3.9 %copy.22 = bf16[8,256,512]{2,1,0:T(8,128)(2,1)} copy(bf16[8,256,512]{1,2,0:T(8,128)(2,1)} %get-tuple-element.6) | data formatting | bytes 4194304 | tf_op jit(solution)/shard_map/jit(_where)/select_n | solution.py:36
  115.0 10.2 %fusion.23 = f32[2048,1536]{1,0:T(8,128)} fusion(bf16[2048,512]{1,0:T(8,128)(2,1)} %bitcast.69, bf16[3,512,1536]{2,1,0:T(8,128)(2,1)} %param.7), kind=kOutput, calls=%fused_computation.33 | convolution fusion | flops 3221225472 | bytes 16252928 | tf_op jit(solution)/shard_map/dot_general | solution.py:35
  125.2 7.8 %fusion.26 = f32[2048,1536]{1,0:T(8,128)} fusion(bf16[2048,512]{1,0:T(8,128)(2,1)S(1)} %bitcast.70, bf16[3,512,1536]{2,1,0:T(8,128)(2,1)} %param.7), kind=kOutput, calls=%fused_computation.36 | convolution fusion | flops 3221225472 | bytes 16252928 | tf_op jit(solution)/shard_map/dot_general | solution.py:35
  133.0 13.3 %add_convert_fusion = bf16[2048,1536]{1,0:T(8,128)(2,1)} fusion(f32[2048,1536]{1,0:T(8,128)} %fusion.26, f32[2048,1536]{1,0:T(8,128)} %fusion.23, bf16[2048,512]{1,0:T(8,128)(2,1)S(1)} %bitcast.65, bf16[3,512,1536]{2,1,0:T(8,128)(2,1)} %param.7), kind=kOutput, calls=%fused_computation | convolution fusion | flops 3230662656 | bytes 35127296 | tf_op jit(solution)/shard_map/dot_general | solution.py:35
  146.4 0.2 reduce-scatter.5.cloned.1.call-start
  146.6 0.0 all-gather.7.cloned.1.call-done
  146.7 6.3 %fusion = f32[2048,512]{1,0:T(8,128)S(1)} fusion(bf16[2048,1536]{1,0:T(8,128)(2,1)} %all-gather.7.cloned.1.call-done, pred[2048]{0:T(1024)(128)(4,1)S(1)} %reshape.57, bf16[3,512,1536]{2,1,0:T(8,128)(2,1)} %param.7), kind=kOutput, calls=%fused_computation.1 | convolution fusion | flops 3224371200 | bytes 12060672 | tf_op jit(solution)/shard_map/dot_general | solution.py:22
  153.0 5.2 %fusion.2 = f32[2048,512]{1,0:T(8,128)S(1)} fusion(bf16[2048,1536]{1,0:T(8,128)(2,1)S(1)} %copy-done.4, pred[2048]{0:T(1024)(128)(4,1)S(1)} %reshape.55, bf16[3,512,1536]{2,1,0:T(8,128)(2,1)} %param.7), kind=kOutput, calls=%fused_computation.3 | convolution fusion | flops 3224371200 | bytes 12060672 | tf_op jit(solution)/shard_map/dot_general | solution.py:22
  158.2 5.2 %add_convert_fusion.1 = bf16[2048,512]{1,0:T(8,128)(2,1)S(1)} fusion(f32[2048,512]{1,0:T(8,128)S(1)} %fusion, f32[2048,512]{1,0:T(8,128)S(1)} %fusion.2, bf16[2048,1536]{1,0:T(8,128)(2,1)S(1)} %copy-done.4, pred[2048]{0:T(1024)(128)(4,1)S(1)} %reshape.53, bf16[3,512,1536]{2,1,0:T(8,128)(2,1)} %param.7), kind=kOutput, calls=%fused_computation.11 | convolution fusion | flops 3227516928 | bytes 18352128 | tf_op jit(solution)/shard_map/dot_general | solution.py:22
  163.4 45.9 %all_to_all.38 = bf16[8,256,512]{2,1,0:T(8,128)(2,1)S(1)} all-to-all(bf16[8,256,512]{2,1,0:T(8,128)(2,1)S(1)} %bitcast.71), channel_id=1, replica_groups=mesh['loop'=8,'tp'=4] {'loop'}, dimensions={0} | all-to-all | bytes 4194304 | tf_op jit(solution)/shard_map/all_to_all | solution.py:31
  209.3 1.6 copy.25
  210.9 2.4 copy.24
  213.3 3.7 %bitcast_select_fusion.2 = (bf16[2048,512]{1,0:T(8,128)(2,1)S(1)}, bf16[2048,512]{1,0:T(8,128)(2,1)S(1)}, bf16[2048,512]{1,0:T(8,128)(2,1)S(1)}) fusion(bf16[8,256,512]{2,1,0:T(8,128)(2,1)} %copy.24, pred[2048]{0:T(1024)(128)(4,1)S(1)} %reshape.53, pred[2048]{0:T(1024)(128)(4,1)S(1)} %reshape.55, pred[2048]{0:T(1024)(128)(4,1)S(1)} %reshape.57), kind=kLoop, calls=%fused_computation.26 | loop fusion | flops 3145728 | bytes 8394752 | tf_op jit(solution)/shard_map/jit(_where)/select_n | solution.py:36
  217.0 6.5 %fusion.15 = bf16[1,512,1536]{2,1,0:T(8,128)(2,1)S(1)} fusion(bf16[2048,512]{1,0:T(8,128)(2,1)S(1)} %get-tuple-element.5, bf16[2048,1536]{1,0:T(8,128)(2,1)} %all-gather.7.cloned.1.call-done), kind=kOutput, calls=%fused_computation.21 | convolution fusion | flops 3222798336 | bytes 9961472 | tf_op jit(solution)/shard_map/dot_general | solution.py:47
  223.5 3.6 %fusion.16 = bf16[1,512,1536]{2,1,0:T(8,128)(2,1)S(1)} fusion(bf16[2048,512]{1,0:T(8,128)(2,1)S(1)} %get-tuple-element.4, bf16[2048,1536]{1,0:T(8,128)(2,1)S(1)} %bitcast.77), kind=kOutput, calls=%fused_computation.22 | convolution fusion | flops 3222798336 | bytes 9961472 | tf_op jit(solution)/shard_map/dot_general | solution.py:47
  227.1 3.6 %fusion.17 = bf16[1,512,1536]{2,1,0:T(8,128)(2,1)S(1)} fusion(bf16[2048,512]{1,0:T(8,128)(2,1)S(1)} %get-tuple-element.3, bf16[2048,1536]{1,0:T(8,128)(2,1)S(1)} %bitcast.77), kind=kOutput, calls=%fused_computation.23 | convolution fusion | flops 3222798336 | bytes 9961472 | tf_op jit(solution)/shard_map/dot_general | solution.py:47
  230.7 2.5 pad_maximum_fusion
  233.2 38.8 %reduce-scatter.5.cloned.1.call-done = bf16[256,1024]{1,0:T(8,128)(2,1)} async-done(((bf16[256,4096]{1,0:T(8,128)(2,1)}), bf16[256,1024]{1,0:T(8,128)(2,1)}) %reduce-scatter.5.cloned.1.call-update) | async-done | bytes 524304 | tf_op jit(solution)/shard_map/reduce_scatter | solution.py:32
  (23 shorter events, 0.1 us)
Async XLA Ops:
  7.2 55.1 %copy-start.2 = (s32[8]{0:T(128)S(1)}, s32[8]{0:T(128)}, u32[]{:S(2)}) copy-start(s32[8]{0:T(128)} %param.9) | copy-start | bytes 100
  7.2 55.8 %copy-start.3 = (s32[256]{0:T(256)S(1)}, s32[256]{0:T(256)}, u32[]{:S(2)}) copy-start(s32[256]{0:T(256)} %param.8) | copy-start | bytes 3076
  7.2 51.4 %all-gather.5.cloned.1.call-start = ((), (), s32[]{:S(2)}) async-start(), calls=%async_computation.4 | async-start | bytes 2621440 | tf_op jit(solution)/shard_map/all_gather | solution.py:17
  9.3 137.4 %all-gather.7.cloned.1.call-start = ((), (), s32[]{:S(2)}) async-start(), calls=%async_computation.6 | async-start | bytes 7077888 | tf_op jit(solution)/shard_map/all_gather | solution.py:16
  58.5 41.8 %all-to-all-start = ((bf16[256,8,512]{0,2,1:T(8,128)(2,1)}), bf16[256,8,512]{0,2,1:T(8,128)(2,1)S(1)}, u32[]{:S(2)}, u32[]{:S(2)}) async-start(bf16[256,8,512]{0,2,1:T(8,128)(2,1)} %bitcast.68), calls=%async_computation | async-start | bytes 4194304 | tf_op jit(solution)/shard_map/all_to_all | solution.py:18
  62.2 171.0 %reduce-scatter.3.cloned.1.call-start = ((), (), s32[]{:S(2)}) async-start(), calls=%async_computation.5 | async-start | bytes 7077888 | tf_op jit(solution)/shard_map/reduce_scatter | solution.py:43
  115.0 10.2 %copy-start.1 = (bf16[8,256,512]{2,1,0:T(8,128)(2,1)S(1)}, bf16[8,256,512]{2,1,0:T(8,128)(2,1)}, u32[]{:S(2)}) copy-start(bf16[8,256,512]{2,1,0:T(8,128)(2,1)} %copy.18) | copy-start | bytes 6291460
  125.2 7.9 %copy-start = (bf16[8,256,512]{2,1,0:T(8,128)(2,1)S(1)}, bf16[8,256,512]{2,1,0:T(8,128)(2,1)}, u32[]{:S(2)}) copy-start(bf16[8,256,512]{2,1,0:T(8,128)(2,1)} %copy.22) | copy-start | bytes 6291460
  146.4 125.6 %reduce-scatter.5.cloned.1.call-start = ((), (), s32[]{:S(2)}) async-start(), calls=%async_computation.7 | async-start | bytes 2621440 | tf_op jit(solution)/shard_map/reduce_scatter | solution.py:32
  146.7 6.3 %copy-start.4 = (bf16[2048,1536]{1,0:T(8,128)(2,1)S(1)}, bf16[2048,1536]{1,0:T(8,128)(2,1)}, u32[]{:S(2)}) copy-start(bf16[2048,1536]{1,0:T(8,128)(2,1)} %all-gather.7.cloned.1.call-done) | copy-start | bytes 18874372
  213.3 10.2 %slice-start = ((s8[6291456]{0:T(1024)(128)(4,1)}), s8[4194304]{0:T(1024)(128)(4,1)S(1)}, s32[]{:S(2)}) async-start(s8[6291456]{0:T(1024)(128)(4,1)} %bitcast.76), calls=%async_computation.8 | async-start | bytes 8388608
  217.0 6.5 %slice-start.1 = ((s8[6291456]{0:T(1024)(128)(4,1)}), s8[2097152]{0:T(1024)(128)(4,1)S(1)}, s32[]{:S(2)}) async-start(s8[6291456]{0:T(1024)(128)(4,1)} %bitcast.76), calls=%async_computation.9 | async-start | bytes 4194304
Sparse Core Ops, SparseCore 0:
  10.1 48.3 all-gather.4
  60.4 58.3 all-gather.6
  146.5 79.0 reduce-scatter.2
  228.3 43.6 reduce-scatter.4
where the time goes:
time: 279 us
  waiting for transfers between devices  88.1 us (32%)
  blocking collectives  78.1 us (28%)
  matrix products  61.7 us (22%)
  local copies, waits for them, and re-layouts  18.6 us (7%)
  other arithmetic  14.1 us (5%)
  between operations  13.9 us (5%)
  starting transfers between devices  3.99 us (1%)
    all_gather x1, waiting for transfers between devices, per_device(): features = lax.all_gather(tokens, 'tp', axis=1, tiled=True)  48.5 us
    all_to_all x1, blocking collectives, per_device(): term = lax.all_to_all(term, 'loop', split_axis=0, concat_axis=1, tiled=True)  45.9 us
    reduce_scatter x1, waiting for transfers between devices, per_device(): input_grad = lax.psum_scatter(term, 'tp', scatter_dimension=1, tiled=True)  38.8 us
    all_gather x1, blocking collectives, per_device(): kind_of = lax.all_gather(own_kind, 'loop', axis=0, tiled=True)  32.2 us
    dot_general x3, matrix products, per_device(): jnp.dot(jnp.where(masks[kind], rows, 0), qkv_weight[kind], preferred_elem...  31.3 us
    dot_general x3, matrix products, per_device(): lax.dot_general(jnp.where(masks[kind], grads, 0), qkv_weight[kind], (((1,...  16.7 us
    dot_general x3, matrix products, per_device(): lax.dot_general(jnp.where(masks[kind], rows, 0), grads, (((0,), (0,)), ((...  13.6 us
    select_n x3, local copies, waits for them, and re-layouts, per_device(): jnp.where(masks[kind], rows, 0)  11.8 us
  transfers between devices with their start and end apart: 5, of which 2 were waited for; matrix products, arithmetic and copies ran while one was open for 33% of the time, Pallas kernels for 0%

commit v1 on v0

--- a/solution.py
+++ b/solution.py
@@ -28,7 +28,19 @@
             for kind in range(kinds)
         )
     ).astype(jnp.bfloat16)
-    term = lax.all_to_all(term, "loop", split_axis=0, concat_axis=1, tiled=True)
+    ways, here = (lax.axis_size("loop"), lax.axis_index("loop"))
+    width = term.shape[0] // ways
+    lengths = list(term.shape)
+    lengths[0] = width
+    height = lengths[1]
+    lengths[1] = height * ways
+    full = jnp.zeros(lengths, term.dtype)
+    for mask in range(ways):
+        part = lax.dynamic_slice_in_dim(term, (here ^ mask) * width, width, axis=0)
+        if mask:
+            part = lax.ppermute(part, "loop", [(d, d ^ mask) for d in range(ways)])
+        full = lax.dynamic_update_slice_in_dim(full, part, (here ^ mask) * height, axis=1)
+    term = full
     input_grad = lax.psum_scatter(term, "tp", scatter_dimension=1, tiled=True)
     partial = sum(
         (

time: 279 us -> 280 us (level)
  blocking collectives: 78.1 us -> 32.3 us
  waiting for transfers between devices: 88.1 us -> 121 us
  local copies, waits for them, and re-layouts: 18.6 us -> 27.7 us
  starting transfers between devices: 3.99 us -> 8.34 us
    all_to_all x1 -> x0, blocking collectives: 45.9 us -> none  [per_device(): term = lax.all_to_all(term, 'loop', split_axis=0, concat_axis=1, tiled=True)]
    ppermute x0 -> x7, waiting for transfers between devices: none -> 30.5 us  [per_device(): part = lax.ppermute(part, 'loop', [(d, d ^ mask) for d in range(ways)])]
    dynamic_update_slice x0 -> x7, local copies, waits for them, and re-layouts: none -> 8.16 us  [per_device(): lax.dynamic_update_slice_in_dim(full, part, (here ^ mask) * height, axis=1)]
    ppermute x0 -> x7, starting transfers between devices: none -> 4.22 us  [per_device(): part = lax.ppermute(part, 'loop', [(d, d ^ mask) for d in range(ways)])]
    reduce_scatter x1, waiting for transfers between devices: 38.8 us -> 41.7 us  [per_device(): input_grad = lax.psum_scatter(term, 'tp', scatter_dimension=1, tiled=True)]
  transfers between devices with their start and end apart: 5 -> 12, of which waited for: 2 -> 7; matrix products, arithmetic and copies ran while one was open for 33% -> 36% of each run, Pallas kernels for 0% -> 0%
where the time goes in v1:
time: 280 us; the launch traced here: 279 us
  waiting for transfers between devices  121 us (43%)
  matrix products  61.6 us (22%)
  blocking collectives  32.3 us (12%)
  local copies, waits for them, and re-layouts  27.7 us (10%)
  other arithmetic  14.1 us (5%)
  between operations  14 us (5%)
  starting transfers between devices  8.34 us (3%)
    all_gather x1, waiting for transfers between devices, per_device(): features = lax.all_gather(tokens, 'tp', axis=1, tiled=True)  48.5 us
    reduce_scatter x1, waiting for transfers between devices, per_device(): input_grad = lax.psum_scatter(term, 'tp', scatter_dimension=1, tiled=True)  41.7 us
    all_gather x1, blocking collectives, per_device(): kind_of = lax.all_gather(own_kind, 'loop', axis=0, tiled=True)  32.3 us
    dot_general x3, matrix products, per_device(): jnp.dot(jnp.where(masks[kind], rows, 0), qkv_weight[kind], preferred_elem...  31.3 us
    ppermute x7, waiting for transfers between devices, per_device(): part = lax.ppermute(part, 'loop', [(d, d ^ mask) for d in range(ways)])  30.5 us
    dot_general x3, matrix products, per_device(): lax.dot_general(jnp.where(masks[kind], grads, 0), qkv_weight[kind], (((1,...  16.7 us
    dot_general x3, matrix products, per_device(): lax.dot_general(jnp.where(masks[kind], rows, 0), grads, (((0,), (0,)), ((...  13.6 us
    select_n x3, local copies, waits for them, and re-layouts, per_device(): jnp.where(masks[kind], rows, 0)  11.8 us
  transfers between devices with their start and end apart: 12, of which 7 were waited for; matrix products, arithmetic and copies ran while one was open for 36% of the time, Pallas kernels for 0%

profile of v1, /device:TPU:0, one launch (start us, length us, event | category | flops | bytes accessed | tf_op | source)
XLA Modules:
  0.0 279.5 jit_solution(1460138987989358045)
XLA Ops:
  7.2 2.0 copy.14
  10.0 48.5 %all-gather.5.cloned.1.call-done = bf16[256,4096]{0,1:T(8,128)(2,1)} async-done(((bf16[256,1024]{0,1:T(8,128)(2,1)}), bf16[256,4096]{0,1:T(8,128)(2,1)}) %all-gather.5.cloned.1.call-update) | async-done | bytes 2097168 | tf_op jit(solution)/shard_map/all_gather | solution.py:17
  58.5 3.8 %all-to-all-start = ((bf16[256,8,512]{0,2,1:T(8,128)(2,1)}), bf16[256,8,512]{0,2,1:T(8,128)(2,1)S(1)}, u32[]{:S(2)}, u32[]{:S(2)}) async-start(bf16[256,8,512]{0,2,1:T(8,128)(2,1)} %bitcast.62), calls=%async_computation | async-start | bytes 4194304 | tf_op jit(solution)/shard_map/all_to_all | solution.py:18
  63.1 5.0 %compare_select_fusion.1 = s32[256]{0:T(256)S(1)} fusion(s32[256]{0:T(256)S(1)} %copy-done.3, s32[]{:T(128)} %bitcast, s32[]{:T(128)} %bitcast.1, s32[]{:T(128)} %bitcast.2, s32[]{:T(128)} %bitcast.3, s32[]{:T(128)} %bitcast.4, s32[]{:T(128)} %bitcast.5, s32[]{:T(128)} %bitcast.6, s32[]{:T(128)} %bitcast.7), kind=kLoop, calls=%fused_computation.63 | loop fusion | flops 6400 | bytes 2080 | tf_op jit(solution)/shard_map/gather | solution.py:14
  68.1 32.3 %all-gather.1 = s32[8,1,256]{2,1,0:T(1,128)S(1)} all-gather(s32[1,1,256]{2,1,0:T(1,128)S(1)} %bitcast.68), channel_id=2, replica_groups=mesh['loop'=8,'tp'=4] {'loop'}, dimensions={0}, use_global_device_ids=true | all-gather | bytes 9216 | tf_op jit(solution)/shard_map/all_gather | solution.py:15
  100.4 2.9 %broadcast_select_fusion = (bf16[8,256,512]{1,2,0:T(8,128)(2,1)}, bf16[8,256,512]{1,2,0:T(8,128)(2,1)}, bf16[8,256,512]{1,2,0:T(8,128)(2,1)}) fusion(pred[8,256]{1,0:T(8,128)(4,1)S(1)} %bitcast.67, bf16[256,8,512]{0,2,1:T(8,128)(2,1)S(1)} %all-to-all-done, pred[8,256]{1,0:T(8,128)(4,1)S(1)} %bitcast.65, pred[8,256]{1,0:T(8,128)(4,1)S(1)} %bitcast.66), kind=kLoop, calls=%fused_computation.27 | loop fusion | flops 3145728 | bytes 8394752 | tf_op jit(solution)/shard_map/jit(_where)/select_n | solution.py:48
  103.3 3.9 %copy.15 = bf16[8,256,512]{2,1,0:T(8,128)(2,1)} copy(bf16[8,256,512]{1,2,0:T(8,128)(2,1)} %get-tuple-element.15) | data formatting | bytes 4194304 | tf_op jit(solution)/shard_map/jit(_where)/select_n | solution.py:48
  107.3 3.9 %copy.17 = bf16[8,256,512]{2,1,0:T(8,128)(2,1)} copy(bf16[8,256,512]{1,2,0:T(8,128)(2,1)} %get-tuple-element.16) | data formatting | bytes 4194304 | tf_op jit(solution)/shard_map/jit(_where)/select_n | solution.py:48
  111.2 3.9 %copy.19 = bf16[8,256,512]{2,1,0:T(8,128)(2,1)} copy(bf16[8,256,512]{1,2,0:T(8,128)(2,1)} %get-tuple-element.14) | data formatting | bytes 4194304 | tf_op jit(solution)/shard_map/jit(_where)/select_n | solution.py:48
  115.1 10.2 %fusion.26 = f32[2048,1536]{1,0:T(8,128)} fusion(bf16[2048,512]{1,0:T(8,128)(2,1)} %bitcast.63, bf16[3,512,1536]{2,1,0:T(8,128)(2,1)} %param.7), kind=kOutput, calls=%fused_computation.36 | convolution fusion | flops 3221225472 | bytes 16252928 | tf_op jit(solution)/shard_map/dot_general | solution.py:47
  125.3 7.9 %fusion.23 = f32[2048,1536]{1,0:T(8,128)} fusion(bf16[2048,512]{1,0:T(8,128)(2,1)S(1)} %bitcast.64, bf16[3,512,1536]{2,1,0:T(8,128)(2,1)} %param.7), kind=kOutput, calls=%fused_computation.33 | convolution fusion | flops 3221225472 | bytes 16252928 | tf_op jit(solution)/shard_map/dot_general | solution.py:47
  133.2 13.3 %add_convert_fusion = bf16[2048,1536]{1,0:T(8,128)(2,1)} fusion(f32[2048,1536]{1,0:T(8,128)} %fusion.26, f32[2048,1536]{1,0:T(8,128)} %fusion.23, bf16[2048,512]{1,0:T(8,128)(2,1)S(1)} %bitcast.61, bf16[3,512,1536]{2,1,0:T(8,128)(2,1)} %param.7), kind=kOutput, calls=%fused_computation | convolution fusion | flops 3230662656 | bytes 35127296 | tf_op jit(solution)/shard_map/dot_general | solution.py:47
  146.8 6.3 %fusion = f32[2048,512]{1,0:T(8,128)S(1)} fusion(bf16[2048,1536]{1,0:T(8,128)(2,1)} %all-gather.7.cloned.1.call-done, pred[2048]{0:T(1024)(128)(4,1)S(1)} %reshape.54, bf16[3,512,1536]{2,1,0:T(8,128)(2,1)} %param.7), kind=kOutput, calls=%fused_computation.1 | convolution fusion | flops 3224371200 | bytes 12060672 | tf_op jit(solution)/shard_map/dot_general | solution.py:22
  153.1 5.2 %fusion.2 = f32[2048,512]{1,0:T(8,128)S(1)} fusion(bf16[2048,1536]{1,0:T(8,128)(2,1)S(1)} %copy-done.4, pred[2048]{0:T(1024)(128)(4,1)S(1)} %reshape.52, bf16[3,512,1536]{2,1,0:T(8,128)(2,1)} %param.7), kind=kOutput, calls=%fused_computation.3 | convolution fusion | flops 3224371200 | bytes 12060672 | tf_op jit(solution)/shard_map/dot_general | solution.py:22
  158.3 5.2 %add_convert_fusion.1 = bf16[2048,512]{1,0:T(8,128)(2,1)S(1)} fusion(f32[2048,512]{1,0:T(8,128)S(1)} %fusion, f32[2048,512]{1,0:T(8,128)S(1)} %fusion.2, bf16[2048,1536]{1,0:T(8,128)(2,1)S(1)} %copy-done.4, pred[2048]{0:T(1024)(128)(4,1)S(1)} %reshape.50, bf16[3,512,1536]{2,1,0:T(8,128)(2,1)} %param.7), kind=kOutput, calls=%fused_computation.11 | convolution fusion | flops 3227516928 | bytes 18352128 | tf_op jit(solution)/shard_map/dot_general | solution.py:22
  163.5 1.6 broadcast_in_dim.91
  166.3 1.6 collective-permute-start.2
  170.3 1.7 constant_dynamic-update-slice_fusion.5
  172.0 9.2 %collective-permute-done.1 = bf16[256,512]{1,0:T(8,128)(2,1)} collective-permute-done((bf16[256,512]{1,0:T(8,128)(2,1)}, bf16[256,512]{1,0:T(8,128)(2,1)}, u32[]{:S(2)}, u32[]{:S(2)}) %collective-permute-start.1) | collective-permute-done | bytes 262176 | tf_op jit(solution)/shard_map/ppermute | solution.py:41
  181.2 1.7 constant_dynamic-update-slice_fusion.4
  182.9 7.5 %collective-permute-done.2 = bf16[256,512]{1,0:T(8,128)(2,1)} collective-permute-done((bf16[256,512]{1,0:T(8,128)(2,1)S(1)}, bf16[256,512]{1,0:T(8,128)(2,1)}, u32[]{:S(2)}, u32[]{:S(2)}) %collective-permute-start.2) | collective-permute-done | bytes 262176 | tf_op jit(solution)/shard_map/ppermute | solution.py:41
  190.4 1.7 constant_dynamic-update-slice_fusion.3
  192.9 2.9 %collective-permute-done.4 = bf16[256,512]{1,0:T(8,128)(2,1)S(1)} collective-permute-done((bf16[256,512]{1,0:T(8,128)(2,1)S(1)}, bf16[256,512]{1,0:T(8,128)(2,1)S(1)}, u32[]{:S(2)}, u32[]{:S(2)}) %collective-permute-start.4) | collective-permute-done | bytes 262176 | tf_op jit(solution)/shard_map/ppermute | solution.py:41
  196.6 6.7 %collective-permute-done.5 = bf16[256,512]{1,0:T(8,128)(2,1)S(1)} collective-permute-done((bf16[256,512]{1,0:T(8,128)(2,1)S(1)}, bf16[256,512]{1,0:T(8,128)(2,1)S(1)}, u32[]{:S(2)}, u32[]{:S(2)}) %collective-permute-start.5) | collective-permute-done | bytes 262176 | tf_op jit(solution)/shard_map/ppermute | solution.py:41
  204.0 4.2 %collective-permute-done.6 = bf16[256,512]{1,0:T(8,128)(2,1)S(1)} collective-permute-done((bf16[256,512]{1,0:T(8,128)(2,1)S(1)}, bf16[256,512]{1,0:T(8,128)(2,1)S(1)}, u32[]{:S(2)}, u32[]{:S(2)}) %collective-permute-start.6) | collective-permute-done | bytes 262176 | tf_op jit(solution)/shard_map/ppermute | solution.py:41
  209.0 2.4 copy.20
  211.4 3.7 %bitcast_select_fusion.2 = (bf16[2048,512]{1,0:T(8,128)(2,1)S(1)}, bf16[2048,512]{1,0:T(8,128)(2,1)S(1)}, bf16[2048,512]{1,0:T(8,128)(2,1)S(1)}) fusion(bf16[8,256,512]{2,1,0:T(8,128)(2,1)} %copy.20, pred[2048]{0:T(1024)(128)(4,1)S(1)} %reshape.50, pred[2048]{0:T(1024)(128)(4,1)S(1)} %reshape.52, pred[2048]{0:T(1024)(128)(4,1)S(1)} %reshape.54), kind=kLoop, calls=%fused_computation.26 | loop fusion | flops 3145728 | bytes 8394752 | tf_op jit(solution)/shard_map/jit(_where)/select_n | solution.py:48
  215.1 6.5 %fusion.15 = bf16[1,512,1536]{2,1,0:T(8,128)(2,1)S(1)} fusion(bf16[2048,512]{1,0:T(8,128)(2,1)S(1)} %get-tuple-element.5, bf16[2048,1536]{1,0:T(8,128)(2,1)} %all-gather.7.cloned.1.call-done), kind=kOutput, calls=%fused_computation.21 | convolution fusion | flops 3222798336 | bytes 9961472 | tf_op jit(solution)/shard_map/dot_general | solution.py:59
  221.6 3.6 %fusion.16 = bf16[1,512,1536]{2,1,0:T(8,128)(2,1)S(1)} fusion(bf16[2048,512]{1,0:T(8,128)(2,1)S(1)} %get-tuple-element.4, bf16[2048,1536]{1,0:T(8,128)(2,1)S(1)} %bitcast.70), kind=kOutput, calls=%fused_computation.22 | convolution fusion | flops 3222798336 | bytes 9961472 | tf_op jit(solution)/shard_map/dot_general | solution.py:59
  225.2 3.6 %fusion.17 = bf16[1,512,1536]{2,1,0:T(8,128)(2,1)S(1)} fusion(bf16[2048,512]{1,0:T(8,128)(2,1)S(1)} %get-tuple-element.3, bf16[2048,1536]{1,0:T(8,128)(2,1)S(1)} %bitcast.70), kind=kOutput, calls=%fused_computation.23 | convolution fusion | flops 3222798336 | bytes 9961472 | tf_op jit(solution)/shard_map/dot_general | solution.py:59
  228.8 2.5 pad_maximum_fusion
  231.2 41.7 %reduce-scatter.5.cloned.1.call-done = bf16[256,1024]{1,0:T(8,128)(2,1)} async-done(((bf16[256,4096]{1,0:T(8,128)(2,1)}), bf16[256,1024]{1,0:T(8,128)(2,1)}) %reduce-scatter.5.cloned.1.call-update) | async-done | bytes 524304 | tf_op jit(solution)/shard_map/reduce_scatter | solution.py:44
  (44 shorter events, 8.5 us)
Async XLA Ops:
  7.2 51.4 %all-gather.5.cloned.1.call-start = ((), (), s32[]{:S(2)}) async-start(), calls=%async_computation.3 | async-start | bytes 2621440 | tf_op jit(solution)/shard_map/all_gather | solution.py:17
  9.3 137.5 %all-gather.7.cloned.1.call-start = ((), (), s32[]{:S(2)}) async-start(), calls=%async_computation.5 | async-start | bytes 7077888 | tf_op jit(solution)/shard_map/all_gather | solution.py:16
  58.5 3.8 %copy-start.2 = (s32[8]{0:T(128)S(1)}, s32[8]{0:T(128)}, u32[]{:S(2)}) copy-start(s32[8]{0:T(128)} %param.9) | copy-start | bytes 100
  58.5 4.5 %copy-start.3 = (s32[256]{0:T(256)S(1)}, s32[256]{0:T(256)}, u32[]{:S(2)}) copy-start(s32[256]{0:T(256)} %param.8) | copy-start | bytes 3076
  58.5 41.9 %all-to-all-start = ((bf16[256,8,512]{0,2,1:T(8,128)(2,1)}), bf16[256,8,512]{0,2,1:T(8,128)(2,1)S(1)}, u32[]{:S(2)}, u32[]{:S(2)}) async-start(bf16[256,8,512]{0,2,1:T(8,128)(2,1)} %bitcast.62), calls=%async_computation | async-start | bytes 4194304 | tf_op jit(solution)/shard_map/all_to_all | solution.py:18
  62.3 168.9 %reduce-scatter.3.cloned.1.call-start = ((), (), s32[]{:S(2)}) async-start(), calls=%async_computation.4 | async-start | bytes 7077888 | tf_op jit(solution)/shard_map/reduce_scatter | solution.py:55
  115.1 10.2 %copy-start.1 = (bf16[8,256,512]{2,1,0:T(8,128)(2,1)S(1)}, bf16[8,256,512]{2,1,0:T(8,128)(2,1)}, u32[]{:S(2)}) copy-start(bf16[8,256,512]{2,1,0:T(8,128)(2,1)} %copy.17) | copy-start | bytes 6291460
  125.3 7.9 %copy-start = (bf16[8,256,512]{2,1,0:T(8,128)(2,1)S(1)}, bf16[8,256,512]{2,1,0:T(8,128)(2,1)}, u32[]{:S(2)}) copy-start(bf16[8,256,512]{2,1,0:T(8,128)(2,1)} %copy.19) | copy-start | bytes 6291460
  146.5 126.5 %reduce-scatter.5.cloned.1.call-start = ((), (), s32[]{:S(2)}) async-start(), calls=%async_computation.6 | async-start | bytes 2621440 | tf_op jit(solution)/shard_map/reduce_scatter | solution.py:44
  146.8 6.3 %copy-start.4 = (bf16[2048,1536]{1,0:T(8,128)(2,1)S(1)}, bf16[2048,1536]{1,0:T(8,128)(2,1)}, u32[]{:S(2)}) copy-start(bf16[2048,1536]{1,0:T(8,128)(2,1)} %all-gather.7.cloned.1.call-done) | copy-start | bytes 18874372
  166.1 3.7 %collective-permute-start = (bf16[256,512]{1,0:T(8,128)(2,1)}, bf16[256,512]{1,0:T(8,128)(2,1)}, u32[]{:S(2)}, u32[]{:S(2)}) collective-permute-start(bf16[256,512]{1,0:T(8,128)(2,1)} %get-tuple-element.12), channel_id=1, source_target_pairs={{0,4},{4,0},{8,12},{12,8},{16,20},{20,16},{24,28},{28,24},{1,5},{5... | collective-permute-start | bytes 786440 | tf_op jit(solution)/shard_map/ppermute | solution.py:41
  166.3 14.9 %collective-permute-start.1 = (bf16[256,512]{1,0:T(8,128)(2,1)}, bf16[256,512]{1,0:T(8,128)(2,1)}, u32[]{:S(2)}, u32[]{:S(2)}) collective-permute-start(bf16[256,512]{1,0:T(8,128)(2,1)} %get-tuple-element.11), channel_id=1, source_target_pairs={{0,8},{4,12},{8,0},{12,4},{16,24},{20,28},{24,16},{28,20},{1,9},{5... | collective-permute-start | bytes 786440 | tf_op jit(solution)/shard_map/ppermute | solution.py:41
  166.3 24.1 %collective-permute-start.2 = (bf16[256,512]{1,0:T(8,128)(2,1)S(1)}, bf16[256,512]{1,0:T(8,128)(2,1)}, u32[]{:S(2)}, u32[]{:S(2)}) collective-permute-start(bf16[256,512]{1,0:T(8,128)(2,1)S(1)} %get-tuple-element.10), channel_id=1, source_target_pairs={{0,12},{4,8},{8,4},{12,0},{16,28},{20,24},{24,20},{28,16},{1,13},{... | collective-permute-start | bytes 786440 | tf_op jit(solution)/shard_map/ppermute | solution.py:41
  168.0 24.1 %collective-permute-start.3 = (bf16[256,512]{1,0:T(8,128)(2,1)S(1)}, bf16[256,512]{1,0:T(8,128)(2,1)S(1)}, u32[]{:S(2)}, u32[]{:S(2)}) collective-permute-start(bf16[256,512]{1,0:T(8,128)(2,1)S(1)} %get-tuple-element.9), channel_id=1, source_target_pairs={{0,16},{4,20},{8,24},{12,28},{16,0},{20,4},{24,8},{28,12},{1,17},{... | collective-permute-start | bytes 786440 | tf_op jit(solution)/shard_map/ppermute | solution.py:41
  168.7 27.2 %collective-permute-start.4 = (bf16[256,512]{1,0:T(8,128)(2,1)S(1)}, bf16[256,512]{1,0:T(8,128)(2,1)S(1)}, u32[]{:S(2)}, u32[]{:S(2)}) collective-permute-start(bf16[256,512]{1,0:T(8,128)(2,1)S(1)} %get-tuple-element.8), channel_id=1, source_target_pairs={{0,20},{4,16},{8,28},{12,24},{16,4},{20,0},{24,12},{28,8},{1,21},{... | collective-permute-start | bytes 786440 | tf_op jit(solution)/shard_map/ppermute | solution.py:41
  169.8 33.4 %collective-permute-start.5 = (bf16[256,512]{1,0:T(8,128)(2,1)S(1)}, bf16[256,512]{1,0:T(8,128)(2,1)S(1)}, u32[]{:S(2)}, u32[]{:S(2)}) collective-permute-start(bf16[256,512]{1,0:T(8,128)(2,1)S(1)} %get-tuple-element.7), channel_id=1, source_target_pairs={{0,24},{4,28},{8,16},{12,20},{16,8},{20,12},{24,0},{28,4},{1,25},{... | collective-permute-start | bytes 786440 | tf_op jit(solution)/shard_map/ppermute | solution.py:41
  181.2 27.0 %collective-permute-start.6 = (bf16[256,512]{1,0:T(8,128)(2,1)S(1)}, bf16[256,512]{1,0:T(8,128)(2,1)S(1)}, u32[]{:S(2)}, u32[]{:S(2)}) collective-permute-start(bf16[256,512]{1,0:T(8,128)(2,1)S(1)} %get-tuple-element.6), channel_id=1, source_target_pairs={{0,28},{4,24},{8,20},{12,16},{16,12},{20,8},{24,4},{28,0},{1,29},{... | collective-permute-start | bytes 786440 | tf_op jit(solution)/shard_map/ppermute | solution.py:41
  211.4 10.2 %slice-start = ((s8[6291456]{0:T(1024)(128)(4,1)}), s8[4194304]{0:T(1024)(128)(4,1)S(1)}, s32[]{:S(2)}) async-start(s8[6291456]{0:T(1024)(128)(4,1)} %bitcast.69), calls=%async_computation.7 | async-start | bytes 8388608
  215.1 6.5 %slice-start.1 = ((s8[6291456]{0:T(1024)(128)(4,1)}), s8[2097152]{0:T(1024)(128)(4,1)S(1)}, s32[]{:S(2)}) async-start(s8[6291456]{0:T(1024)(128)(4,1)} %bitcast.69), calls=%async_computation.8 | async-start | bytes 4194304
Sparse Core Ops, SparseCore 0:
  10.1 48.3 all-gather.4
  60.4 58.3 all-gather.6
  146.6 79.9 reduce-scatter.2
  229.3 43.6 reduce-scatter.4
